TPU v7x, 32 devices: a whole 2x2x4 slice. The times are simulated.
32 devices in a mesh: ctx: 8 (over z, x), exp: 4 (over y, core).
Axes of the slice: x: 2, y: 2, z: 4, core: 2. Of those that a mesh axis runs over, the one named last changes fastest.
Arguments:
- tokens: bfloat16 [2, 1024, 4096], P(None, 'ctx'), may hold values from -1.5 to 1.5
- router: bfloat16 [4096, 2048], P('ctx', 'exp'), may hold values from -8 to 8
- slot_out: bfloat16 [2, 2048, 4096], P(None, 'exp', 'ctx'), may hold values from -6 to 6
- out_grad: bfloat16 [2, 1024, 4096], P(None, 'ctx'), may hold values from -3 to 3
- slot_in_grad: bfloat16 [2, 2048, 4096], P(None, 'exp', 'ctx'), may hold values from -60 to 60
- lengths: int32 [2], replicated, may hold values from 256 to 1024, as said below
Outputs:
- grad_tokens: bfloat16 [2, 1024, 4096], P(None, 'ctx', 'exp')
- grad_router: float32 [4096, 2048], P('ctx', 'exp')
Inputs may be any that keep to these rules, and one draw needn't show every extreme that they name: `lengths`: at least one sequence is valid at all 1024 positions.
All inputs are finite; a program needn't handle non-finite values.
Results may differ from a plain program's by a relative error of at most 0.017.
Values may be sent and summed in bfloat16 or wider, within the bound.
No kernel may reach another device: no remote copies, remote signals or barrier semaphores. Data moves between devices by JAX's collectives and lax.ppermute only.
A program may use at most 64 MiB of HBM per device.

v0:
```python
import jax
import jax.numpy as jnp
from jax import lax
from jax.sharding import PartitionSpec as P

masked_logit = -1e30


def local(tokens, router, slot_out, out_grad, slot_in_grad, lengths):
    seq_count, tok_rows, model_width = tokens.shape
    local_slots = router.shape[1]
    start_row = lax.axis_index("ctx") * tok_rows
    positions = start_row + jnp.arange(tok_rows, dtype=jnp.int32)
    valid_mask = positions[None, :] < lengths[:, None]
    router_full = lax.all_gather(router, "ctx", axis=0, tiled=True)
    flat_tokens = tokens.reshape(seq_count * tok_rows, model_width)
    logits = jnp.dot(flat_tokens, router_full, preferred_element_type=jnp.float32).reshape(
        seq_count, tok_rows, local_slots
    )
    grad_in = jnp.where(valid_mask[:, :, None], out_grad, jnp.zeros((), out_grad.dtype))
    comb_grad = jnp.einsum(
        "bnd,bsd->bns",
        grad_in,
        lax.all_gather(slot_out, "ctx", axis=2, tiled=True),
        preferred_element_type=jnp.float32,
    )
    grads_full = lax.all_gather(slot_in_grad, "ctx", axis=2, tiled=True)
    disp_grad = jnp.einsum("bnd,bsd->bns", tokens, grads_full, preferred_element_type=jnp.float32)
    local_peak = jnp.max(logits, axis=2)
    shifted = jnp.exp(logits - local_peak[:, :, None])
    local_total = jnp.sum(shifted, axis=2)
    local_weighted = jnp.sum(shifted * comb_grad, axis=2)
    masked = jnp.where(valid_mask[:, :, None], logits, masked_logit)
    slot_peak = jnp.max(masked, axis=1)
    slot_shift = jnp.where(valid_mask[:, :, None], jnp.exp(masked - slot_peak[:, None, :]), 0.0)
    slot_total = jnp.sum(slot_shift, axis=1)
    slot_weighted = jnp.sum(slot_shift * disp_grad, axis=1)
    comb_peak = lax.pmax(local_peak, "exp")
    disp_peak = lax.pmax(slot_peak, "ctx")
    comb_rescale = jnp.exp(local_peak - comb_peak)
    comb_total, comb_weighted = lax.psum(
        (local_total * comb_rescale, local_weighted * comb_rescale), "exp"
    )
    disp_rescale = jnp.exp(slot_peak - disp_peak)
    disp_total, disp_weighted = lax.psum(
        (slot_total * disp_rescale, slot_weighted * disp_rescale), "ctx"
    )
    combine = jnp.exp(logits - comb_peak[:, :, None]) / comb_total[:, :, None]
    comb_mean = comb_weighted / comb_total
    dispatch = jnp.where(
        valid_mask[:, :, None],
        jnp.exp(masked - disp_peak[:, None, :]) / disp_total[:, None, :],
        0.0,
    )
    disp_mean = disp_weighted / disp_total
    grad_logits = combine * (comb_grad - comb_mean[:, :, None]) + dispatch * (
        disp_grad - disp_mean[:, None, :]
    )
    logit_low = grad_logits.astype(jnp.bfloat16)
    dispatch_low = dispatch.astype(jnp.bfloat16)

    def router_term(amount):
        running = jnp.zeros((amount, local_slots), jnp.float32)
        for seq_index in range(seq_count):

            def compute(seq_index=seq_index):
                return jnp.einsum(
                    "nd,ns->ds",
                    tokens[seq_index],
                    logit_low[seq_index],
                    preferred_element_type=jnp.float32,
                )

            running = running + compute()
        return running

    grad_router = lax.psum_scatter(
        router_term(router.shape[0] * lax.axis_size("ctx")).astype(jnp.bfloat16),
        "ctx",
        scatter_dimension=0,
        tiled=True,
    ).astype(jnp.float32)
    blocks = []
    for seq_index in range(seq_count):

        def compute(seq_index=seq_index):
            first = jnp.dot(
                dispatch_low[seq_index], grads_full[seq_index], preferred_element_type=jnp.float32
            )
            return first + jnp.einsum(
                "ns,ds->nd", logit_low[seq_index], router_full, preferred_element_type=jnp.float32
            )

        blocks.append(compute())
    partial_grad = jnp.stack(blocks)
    grad_tokens = lax.psum_scatter(
        partial_grad.astype(jnp.bfloat16), "exp", scatter_dimension=2, tiled=True
    )
    return (grad_tokens, grad_router)


def solution(mesh):
    return jax.shard_map(
        local,
        mesh=mesh,
        in_specs=(
            P(None, "ctx", None),
            P("ctx", "exp"),
            P(None, "exp", "ctx"),
            P(None, "ctx", None),
            P(None, "exp", "ctx"),
            P(),
        ),
        out_specs=(P(None, "ctx", "exp"), P("ctx", "exp")),
        check_vma=False,
    )
```

profile of v0, /device:TPU:0, one launch (start us, length us, event | category | flops | bytes accessed | tf_op | source)
XLA Modules:
  0.0 502.1 jit_solution(17626797504241054919)
XLA Ops:
  7.2 0.7 all-gather.4.cloned.1.call-update
  7.9 0.7 all-gather.6.cloned.1.call-update
  9.4 0.7 broadcast_compare_fusion
  10.2 75.5 %all-gather.4.cloned.1.call-done = bf16[4096,512]{1,0:T(8,128)(2,1)} async-done(((bf16[512,512]{1,0:T(8,128)(2,1)}), bf16[4096,512]{1,0:T(8,128)(2,1)}) %all-gather.4.cloned.1.call-update) | async-done | bytes 4194320 | tf_op jit(solution)/shard_map/all_gather | solution.py:15
  85.6 4.2 fusion.26
  89.8 5.7 %pmax.15 = f32[2,128]{1,0:T(2,128)S(1)} all-reduce(f32[2,128]{1,0:T(2,128)S(1)} %get-tuple-element.10), channel_id=1, replica_groups=mesh['ctx'=8,'exp'=4] {'exp'}, use_global_device_ids=true, to_apply=%region_5.6 | all-reduce | flops 256 | bytes 2048 | tf_op jit(solution)/shard_map/pmax | solution.py:38
  95.5 20.5 %pmax.14 = f32[2,512]{1,0:T(2,128)S(1)} all-reduce(f32[2,512]{1,0:T(2,128)S(1)} %get-tuple-element.11), channel_id=1, replica_groups=mesh['ctx'=8,'exp'=4] {'ctx'}, use_global_device_ids=true, to_apply=%region_1.2 | all-reduce | flops 1024 | bytes 8192 | tf_op jit(solution)/shard_map/pmax | solution.py:39
  116.0 95.7 %all-gather.6.cloned.1.call-done = bf16[2,512,4096]{2,1,0:T(8,128)(2,1)} async-done(((bf16[2,512,512]{2,1,0:T(8,128)(2,1)}), bf16[2,512,4096]{2,1,0:T(8,128)(2,1)}) %all-gather.6.cloned.1.call-update) | async-done | bytes 8388624 | tf_op jit(solution)/shard_map/all_gather | solution.py:27
  211.7 6.3 %fusion.27 = f32[2,128,512]{2,1,0:T(8,128)S(1)} fusion(bf16[2,128,4096]{2,1,0:T(8,128)(2,1)S(1)} %copy-done.1, bf16[2,512,4096]{2,1,0:T(8,128)(2,1)} %all-gather.6.cloned.1.call-done), kind=kOutput, calls=%fused_computation.48 | convolution fusion | flops 1073741824 | bytes 11010048 | tf_op jit(solution)/shard_map/bnd,bsd->bns/dot_general | solution.py:28
  218.0 118.9 %all-gather.8.cloned.1.call-done = bf16[2,512,4096]{2,1,0:T(8,128)(2,1)} async-done(((bf16[2,512,512]{2,1,0:T(8,128)(2,1)}), bf16[2,512,4096]{2,1,0:T(8,128)(2,1)}) %all-gather.8.cloned.1.call-update) | async-done | bytes 8388624 | tf_op jit(solution)/shard_map/all_gather | solution.py:24
  336.9 7.8 %fusion.18 = (f32[2,128]{1,0:T(2,128)S(1)}, f32[2,128]{1,0:T(2,128)S(1)}, f32[2,512]{1,0:T(2,128)S(1)}, f32[2,512]{1,0:T(2,128)S(1)}, f32[2,128,512]{2,1,0:T(8,128)}) fusion(f32[2,128,512]{2,1,0:T(8,128)S(1)} %get-tuple-element.22, f32[2,128]{1,0:T(2,128)S(1)} %get-tuple-element.10, f32[2,512]{1,0:T(2,128)S(1)} %get-tuple-element.11, ...), kind=kOutput, calls=%fused_computation.30 | convolution fusion | flops 1076098560 | bytes 12074240 | tf_op jit(solution)/shard_map/bnd,bsd->bns/dot_general | solution.py:21
  344.7 5.9 %all-reduce.1 = (f32[2,128]{1,0:T(2,128)S(1)}, f32[2,128]{1,0:T(2,128)S(1)}) all-reduce(f32[2,128]{1,0:T(2,128)S(1)} %get-tuple-element.21, f32[2,128]{1,0:T(2,128)S(1)} %get-tuple-element.20), channel_id=1, replica_groups=mesh['ctx'=8,'exp'=4] {'exp'}, use_global_device_ids=true, to_apply=%region_9.10 | all-reduce | flops 512 | bytes 4096 | tf_op jit(solution)/shard_map/psum | solution.py:41
  350.6 19.8 %all-reduce = (f32[2,512]{1,0:T(2,128)S(1)}, f32[2,512]{1,0:T(2,128)S(1)}) all-reduce(f32[2,512]{1,0:T(2,128)S(1)} %get-tuple-element.19, f32[2,512]{1,0:T(2,128)S(1)} %get-tuple-element.18), channel_id=1, replica_groups=mesh['ctx'=8,'exp'=4] {'ctx'}, use_global_device_ids=true, to_apply=%region_11.12 | all-reduce | flops 2048 | bytes 16384 | tf_op jit(solution)/shard_map/psum | solution.py:45
  370.4 1.6 add_convert_fusion.1
  372.0 1.3 fusion.13
  373.3 3.3 fusion
  376.6 2.9 fusion.5
  379.5 3.3 fusion.6
  383.3 1.5 fusion.4
  384.8 1.5 fusion.3
  386.3 1.5 pad_maximum_fusion
  387.8 74.0 %reduce-scatter.5.cloned.1.call-done = bf16[512,512]{0,1:T(8,128)(2,1)} async-done(((bf16[4096,512]{0,1:T(8,128)(2,1)}), bf16[512,512]{0,1:T(8,128)(2,1)}) %reduce-scatter.5.cloned.1.call-update) | async-done | bytes 524304 | tf_op jit(solution)/shard_map/reduce_scatter | solution.py:77
  461.8 2.2 copy.8
  464.0 31.6 %reduce-scatter.3.cloned.1.call-done = bf16[2,128,1024]{2,1,0:T(8,128)(2,1)} async-done(((bf16[2,128,4096]{2,1,0:T(8,128)(2,1)}), bf16[2,128,1024]{2,1,0:T(8,128)(2,1)}) %reduce-scatter.3.cloned.1.call-update) | async-done | bytes 524304 | tf_op jit(solution)/shard_map/reduce_scatter | solution.py:96
  (19 shorter events, 1.4 us)
Async XLA Ops:
  7.2 78.5 %all-gather.4.cloned.1.call-start = ((), (), s32[]{:S(2)}) async-start(), calls=%async_computation.2 | async-start | bytes 4718592 | tf_op jit(solution)/shard_map/all_gather | solution.py:15
  7.9 203.8 %all-gather.6.cloned.1.call-start = ((), (), s32[]{:S(2)}) async-start(), calls=%async_computation.3 | async-start | bytes 9437184 | tf_op jit(solution)/shard_map/all_gather | solution.py:27
  8.6 328.3 %all-gather.8.cloned.1.call-start = ((), (), s32[]{:S(2)}) async-start(), calls=%async_computation.4 | async-start | bytes 9437184 | tf_op jit(solution)/shard_map/all_gather | solution.py:24
  9.4 452.4 %reduce-scatter.5.cloned.1.call-start = ((), (), s32[]{:S(2)}) async-start(), calls=%async_computation.6 | async-start | bytes 4718592 | tf_op jit(solution)/shard_map/reduce_scatter | solution.py:77
  10.2 201.5 %copy-start.1 = (bf16[2,128,4096]{2,1,0:T(8,128)(2,1)S(1)}, bf16[2,128,4096]{2,1,0:T(8,128)(2,1)}, u32[]{:S(2)}) copy-start(bf16[2,128,4096]{2,1,0:T(8,128)(2,1)} %param.6) | copy-start | bytes 6291460
  89.8 247.1 %copy-start.2 = (f32[2,128,512]{2,1,0:T(8,128)}, f32[2,128,512]{2,1,0:T(8,128)S(1)}, u32[]{:S(2)}) copy-start(f32[2,128,512]{2,1,0:T(8,128)S(1)} %get-tuple-element.22) | copy-start | bytes 1572868
  376.6 119.0 %reduce-scatter.3.cloned.1.call-start = ((), (), s32[]{:S(2)}) async-start(), calls=%async_computation.5 | async-start | bytes 2621440 | tf_op jit(solution)/shard_map/reduce_scatter | solution.py:96
  379.5 3.7 copy-start
Sparse Core Ops, SparseCore 0:
  10.1 75.4 all-gather.3
  87.7 123.9 all-gather.5
  213.8 123.1 all-gather.7
  376.7 85.0 reduce-scatter.4
  464.8 30.8 reduce-scatter.2
where the time goes:
time: 502 us
  waiting for transfers between devices  398 us (79%)
  blocking collectives  51.9 us (10%)
  matrix products  31.9 us (6%)
  between operations  13.9 us (3%)
    all_gather x1, waiting for transfers between devices, local(): lax.all_gather(slot_out, 'ctx', axis=2, tiled=True)  119 us
    all_gather x1, waiting for transfers between devices, local(): grads_full = lax.all_gather(slot_in_grad, 'ctx', axis=2, tiled=True)  95.7 us
    all_gather x1, waiting for transfers between devices, local(): router_full = lax.all_gather(router, 'ctx', axis=0, tiled=True)  75.5 us
    reduce_scatter x1, waiting for transfers between devices, local(): lax.psum_scatter(router_term(router.shape[0] * lax.axis_size('ctx')).asty...  74 us
    reduce_scatter x1, waiting for transfers between devices, local(): lax.psum_scatter(partial_grad.astype(jnp.bfloat16), 'exp', scatter_dimens...  31.6 us
    pmax x1, blocking collectives, local(): disp_peak = lax.pmax(slot_peak, 'ctx')  20.5 us
    psum x1, blocking collectives, local(): lax.psum((slot_total * disp_rescale, slot_weighted * disp_rescale), 'ctx')  19.8 us
  transfers between devices with their start and end apart: 5, of which 5 were waited for; matrix products, arithmetic and copies ran while one was open for 5% of the time, Pallas kernels for 0%

commit v1 on v0

--- a/solution.py
+++ b/solution.py
@@ -12,7 +12,12 @@
     start_row = lax.axis_index("ctx") * tok_rows
     positions = start_row + jnp.arange(tok_rows, dtype=jnp.int32)
     valid_mask = positions[None, :] < lengths[:, None]
-    router_full = lax.all_gather(router, "ctx", axis=0, tiled=True)
+    ring = [router]
+    for hop in range(7):
+        ring.append(lax.ppermute(ring[-1], "ctx", [(dev, (dev + 1) % 8) for dev in range(8)]))
+    router_full = jnp.roll(
+        jnp.concatenate(ring[::-1], axis=0), (lax.axis_index("ctx") + 1) * ring[0].shape[0], axis=0
+    )
     flat_tokens = tokens.reshape(seq_count * tok_rows, model_width)
     logits = jnp.dot(flat_tokens, router_full, preferred_element_type=jnp.float32).reshape(
         seq_count, tok_rows, local_slots

time: 502 us -> 471 us (0.938)
  waiting for transfers between devices: 398 us -> 320 us
  starting transfers between devices: 0.19 us -> 19.3 us
  blocking collectives: 51.9 us -> 66.7 us
  local copies, waits for them, and re-layouts: 2.69 us -> 15.2 us
    ppermute x0 -> x7, waiting for transfers between devices: none -> 157 us  [local(): lax.ppermute(ring[-1], 'ctx', [(dev, (dev + 1) % 8) for dev in range(8)])]
    all_gather x1, waiting for transfers between devices: 95.7 us -> 0.02 us  [local(): grads_full = lax.all_gather(slot_in_grad, 'ctx', axis=2, tiled=True)]
    all_gather x1 -> x0, waiting for transfers between devices: 75.5 us -> none  [local(): router_full = lax.all_gather(router, 'ctx', axis=0, tiled=True)]
    all_gather x1, waiting for transfers between devices: 119 us -> 56.3 us  [local(): lax.all_gather(slot_out, 'ctx', axis=2, tiled=True)]
    ppermute x0 -> x7, starting transfers between devices: none -> 19 us  [local(): lax.ppermute(ring[-1], 'ctx', [(dev, (dev + 1) % 8) for dev in range(8)])]
    pmax x1, blocking collectives: 20.5 us -> 34.9 us  [local(): disp_peak = lax.pmax(slot_peak, 'ctx')]
    unnamed x7 -> x46, local copies, waits for them, and re-layouts: 2.69 us -> 15.2 us
  transfers between devices with their start and end apart: 5 -> 11, of which waited for: 5 -> 10; matrix products, arithmetic and copies ran while one was open for 5% -> 7% of each run, Pallas kernels for 0% -> 0%
where the time goes in v1:
time: 471 us
  waiting for transfers between devices  320 us (68%)
  blocking collectives  66.7 us (14%)
  matrix products  30.5 us (6%)
  starting transfers between devices  19.3 us (4%)
  local copies, waits for them, and re-layouts  15.2 us (3%)
  between operations  14.1 us (3%)
  other arithmetic  4.98 us (1%)
    ppermute x7, waiting for transfers between devices, local(): lax.ppermute(ring[-1], 'ctx', [(dev, (dev + 1) % 8) for dev in range(8)])  157 us
    reduce_scatter x1, waiting for transfers between devices, local(): lax.psum_scatter(router_term(router.shape[0] * lax.axis_size('ctx')).asty...  73.7 us
    all_gather x1, waiting for transfers between devices, local(): lax.all_gather(slot_out, 'ctx', axis=2, tiled=True)  56.3 us
    pmax x1, blocking collectives, local(): disp_peak = lax.pmax(slot_peak, 'ctx')  34.9 us
    reduce_scatter x1, waiting for transfers between devices, local(): lax.psum_scatter(partial_grad.astype(jnp.bfloat16), 'exp', scatter_dimens...  31.6 us
    psum x1, blocking collectives, local(): lax.psum((slot_total * disp_rescale, slot_weighted * disp_rescale), 'ctx')  20.1 us
    ppermute x7, starting transfers between devices, local(): lax.ppermute(ring[-1], 'ctx', [(dev, (dev + 1) % 8) for dev in range(8)])  19 us
    unnamed x46, local copies, waits for them, and re-layouts  15.2 us
  transfers between devices with their start and end apart: 11, of which 10 were waited for; matrix products, arithmetic and copies ran while one was open for 7% of the time, Pallas kernels for 0%

profile of v1, /device:TPU:0, one launch (start us, length us, event | category | flops | bytes accessed | tf_op | source)
XLA Modules:
  0.0 470.5 jit_solution(7663898905694833167)
XLA Ops:
  8.7 3.0 collective-permute-start
  11.7 15.3 %collective-permute-done = bf16[512,512]{1,0:T(8,128)(2,1)S(1)} collective-permute-done((bf16[512,512]{1,0:T(8,128)(2,1)}, bf16[512,512]{1,0:T(8,128)(2,1)S(1)}, u32[]{:S(2)}, u32[]{:S(2)}) %collective-permute-start) | collective-permute-done | bytes 524320 | tf_op jit(solution)/shard_map/ppermute | solution.py:17
  28.2 22.6 %collective-permute-done.1 = bf16[512,512]{1,0:T(8,128)(2,1)S(1)} collective-permute-done((bf16[512,512]{1,0:T(8,128)(2,1)S(1)}, bf16[512,512]{1,0:T(8,128)(2,1)S(1)}, u32[]{:S(2)}, u32[]{:S(2)}) %collective-permute-start.1) | collective-permute-done | bytes 524320 | tf_op jit(solution)/shard_map/ppermute | solution.py:17
  50.8 27.9 %collective-permute-done.2 = bf16[512,512]{1,0:T(8,128)(2,1)S(1)} collective-permute-done((bf16[512,512]{1,0:T(8,128)(2,1)S(1)}, bf16[512,512]{1,0:T(8,128)(2,1)S(1)}, u32[]{:S(2)}, u32[]{:S(2)}) %collective-permute-start.2) | collective-permute-done | bytes 524320 | tf_op jit(solution)/shard_map/ppermute | solution.py:17
  78.7 18.3 %collective-permute-done.3 = bf16[512,512]{1,0:T(8,128)(2,1)S(1)} collective-permute-done((bf16[512,512]{1,0:T(8,128)(2,1)S(1)}, bf16[512,512]{1,0:T(8,128)(2,1)S(1)}, u32[]{:S(2)}, u32[]{:S(2)}) %collective-permute-start.3) | collective-permute-done | bytes 524320 | tf_op jit(solution)/shard_map/ppermute | solution.py:17
  97.0 27.3 %collective-permute-done.4 = bf16[512,512]{1,0:T(8,128)(2,1)S(1)} collective-permute-done((bf16[512,512]{1,0:T(8,128)(2,1)S(1)}, bf16[512,512]{1,0:T(8,128)(2,1)S(1)}, u32[]{:S(2)}, u32[]{:S(2)}) %collective-permute-start.4) | collective-permute-done | bytes 524320 | tf_op jit(solution)/shard_map/ppermute | solution.py:17
  124.9 27.0 %collective-permute-done.5 = bf16[512,512]{1,0:T(8,128)(2,1)} collective-permute-done((bf16[512,512]{1,0:T(8,128)(2,1)S(1)}, bf16[512,512]{1,0:T(8,128)(2,1)}, u32[]{:S(2)}, u32[]{:S(2)}) %collective-permute-start.5) | collective-permute-done | bytes 524320 | tf_op jit(solution)/shard_map/ppermute | solution.py:17
  151.9 14.3 %collective-permute-start.6 = (bf16[512,512]{1,0:T(8,128)(2,1)}, bf16[512,512]{1,0:T(8,128)(2,1)}, u32[]{:S(2)}, u32[]{:S(2)}) collective-permute-start(bf16[512,512]{1,0:T(8,128)(2,1)} %collective-permute-done.5), channel_id=1, source_target_pairs={{0,4},{4,8},{8,12},{12,16},{16,20},{20,24},{24,28},{28,0},{1,5},{5... | collective-permute-start | bytes 1572872 | tf_op jit(solution)/shard_map/ppermute | solution.py:17
  166.9 18.3 %collective-permute-done.6 = bf16[512,512]{1,0:T(8,128)(2,1)} collective-permute-done((bf16[512,512]{1,0:T(8,128)(2,1)}, bf16[512,512]{1,0:T(8,128)(2,1)}, u32[]{:S(2)}, u32[]{:S(2)}) %collective-permute-start.6) | collective-permute-done | bytes 524320 | tf_op jit(solution)/shard_map/ppermute | solution.py:17
  194.3 3.2 copy-done
  198.9 5.7 %pmax.15 = f32[2,128]{1,0:T(2,128)S(1)} all-reduce(f32[2,128]{1,0:T(2,128)S(1)} %bitcast.59), channel_id=1, replica_groups=mesh['ctx'=8,'exp'=4] {'exp'}, use_global_device_ids=true, to_apply=%region_5.6 | all-reduce | flops 256 | bytes 2048 | tf_op jit(solution)/shard_map/pmax | solution.py:43
  204.5 34.9 %pmax.14 = f32[2,512]{1,0:T(2,128)S(1)} all-reduce(f32[2,512]{1,0:T(2,128)S(1)} %get-tuple-element.16), channel_id=1, replica_groups=mesh['ctx'=8,'exp'=4] {'ctx'}, use_global_device_ids=true, to_apply=%region_1.2 | all-reduce | flops 1024 | bytes 8192 | tf_op jit(solution)/shard_map/pmax | solution.py:44
  239.7 6.3 %multiply_reduce_fusion = (f32[2,512]{1,0:T(2,128)S(1)}, f32[2,512]{1,0:T(2,128)S(1)}, f32[2,128,512]{2,1,0:T(8,128)S(1)}) fusion(f32[2,512]{1,0:T(2,128)S(1)} %get-tuple-element.16, pred[2,128]{1,0:T(4,128)(4,1)S(1)} %broadcast_compare_fusion, f32[512,256]{0,1:T(8,128)S(1)} %get-tuple-element.17, bf16[2,128,4096]{2,1,0:T(8,128)(2,1)S(1)} %copy-done.1, ...), kind=kOutput, calls=%fused_computation.30 | convolution fusion | flops 1074526208 | bytes 11546880 | tf_op jit(solution)/shard_map/bnd,bsd->bns/dot_general | solution.py:33
  246.0 20.1 %all-reduce = (f32[2,512]{1,0:T(2,128)S(1)}, f32[2,512]{1,0:T(2,128)S(1)}) all-reduce(f32[2,512]{1,0:T(2,128)S(1)} %get-tuple-element.13, f32[2,512]{1,0:T(2,128)S(1)} %get-tuple-element.12), channel_id=1, replica_groups=mesh['ctx'=8,'exp'=4] {'ctx'}, use_global_device_ids=true, to_apply=%region_11.12 | all-reduce | flops 2048 | bytes 16384 | tf_op jit(solution)/shard_map/psum | solution.py:50
  266.1 56.3 %all-gather.5.cloned.1.call-done = bf16[2,512,4096]{2,1,0:T(8,128)(2,1)} async-done(((bf16[2,512,512]{2,1,0:T(8,128)(2,1)}), bf16[2,512,4096]{2,1,0:T(8,128)(2,1)}) %all-gather.5.cloned.1.call-update) | async-done | bytes 8388624 | tf_op jit(solution)/shard_map/all_gather | solution.py:29
  322.4 6.9 %fusion.11 = f32[2,128,512]{2,1,0:T(8,128)S(1)} fusion(bf16[2,512,4096]{2,1,0:T(8,128)(2,1)} %all-gather.5.cloned.1.call-done, bf16[2,128,4096]{2,1,0:T(8,128)(2,1)} %param.9, pred[2,128]{1,0:T(4,128)(4,1)S(1)} %broadcast_compare_fusion), kind=kOutput, calls=%fused_computation.17 | convolution fusion | flops 1074790400 | bytes 11010304 | tf_op jit(solution)/shard_map/bnd,bsd->bns/dot_general | solution.py:26
  330.4 6.1 %all-reduce.1 = (f32[2,128]{1,0:T(2,128)S(1)}, f32[2,128]{1,0:T(2,128)S(1)}) all-reduce(f32[2,128]{1,0:T(2,128)S(1)} %get-tuple-element.15, f32[2,128]{1,0:T(2,128)S(1)} %get-tuple-element.14), channel_id=1, replica_groups=mesh['ctx'=8,'exp'=4] {'exp'}, use_global_device_ids=true, to_apply=%region_9.10 | all-reduce | flops 512 | bytes 4096 | tf_op jit(solution)/shard_map/psum | solution.py:46
  339.9 3.3 fusion
  343.4 3.1 fusion.5
  346.5 4.0 fusion.3
  350.5 2.9 fusion.6
  356.5 73.7 %reduce-scatter.5.cloned.1.call-done = bf16[512,512]{0,1:T(8,128)(2,1)} async-done(((bf16[4096,512]{0,1:T(8,128)(2,1)}), bf16[512,512]{0,1:T(8,128)(2,1)}) %reduce-scatter.5.cloned.1.call-update) | async-done | bytes 524304 | tf_op jit(solution)/shard_map/reduce_scatter | solution.py:82
  430.2 2.2 copy.8
  432.4 31.6 %reduce-scatter.3.cloned.1.call-done = bf16[2,128,1024]{2,1,0:T(8,128)(2,1)} async-done(((bf16[2,128,4096]{2,1,0:T(8,128)(2,1)}), bf16[2,128,1024]{2,1,0:T(8,128)(2,1)}) %reduce-scatter.3.cloned.1.call-update) | async-done | bytes 524304 | tf_op jit(solution)/shard_map/reduce_scatter | solution.py:101
  (74 shorter events, 22.2 us)
Async XLA Ops:
  7.2 184.6 %copy-start.3 = (bf16[512,512]{1,0:T(8,128)(2,1)S(1)}, bf16[512,512]{1,0:T(8,128)(2,1)}, u32[]{:S(2)}) copy-start(bf16[512,512]{1,0:T(8,128)(2,1)} %param.7) | copy-start | bytes 1572868
  7.2 232.5 %all-gather.3.cloned.1.call-start = ((), (), s32[]{:S(2)}) async-start(), calls=%async_computation.2 | async-start | bytes 9437184 | tf_op jit(solution)/shard_map/all_gather | solution.py:32
  7.9 314.5 %all-gather.5.cloned.1.call-start = ((), (), s32[]{:S(2)}) async-start(), calls=%async_computation.3 | async-start | bytes 9437184 | tf_op jit(solution)/shard_map/all_gather | solution.py:29
  8.7 421.5 %reduce-scatter.5.cloned.1.call-start = ((), (), s32[]{:S(2)}) async-start(), calls=%async_computation.5 | async-start | bytes 4718592 | tf_op jit(solution)/shard_map/reduce_scatter | solution.py:82
  8.7 18.3 %collective-permute-start = (bf16[512,512]{1,0:T(8,128)(2,1)}, bf16[512,512]{1,0:T(8,128)(2,1)S(1)}, u32[]{:S(2)}, u32[]{:S(2)}) collective-permute-start(bf16[512,512]{1,0:T(8,128)(2,1)} %param.7), channel_id=1, source_target_pairs={{0,4},{4,8},{8,12},{12,16},{16,20},{20,24},{24,28},{28,0},{1,5},{5... | collective-permute-start | bytes 1572872 | tf_op jit(solution)/shard_map/ppermute | solution.py:17
  27.0 23.8 %collective-permute-start.1 = (bf16[512,512]{1,0:T(8,128)(2,1)S(1)}, bf16[512,512]{1,0:T(8,128)(2,1)S(1)}, u32[]{:S(2)}, u32[]{:S(2)}) collective-permute-start(bf16[512,512]{1,0:T(8,128)(2,1)S(1)} %collective-permute-done), channel_id=1, source_target_pairs={{0,4},{4,8},{8,12},{12,16},{16,20},{20,24},{24,28},{28,0},{1,5},{5... | collective-permute-start | bytes 1572872 | tf_op jit(solution)/shard_map/ppermute | solution.py:17
  50.8 115.4 %copy-start.4 = (bf16[512,512]{1,0:T(8,128)(2,1)}, bf16[512,512]{1,0:T(8,128)(2,1)S(1)}, u32[]{:S(2)}) copy-start(bf16[512,512]{1,0:T(8,128)(2,1)S(1)} %collective-permute-done.1) | copy-start | bytes 1572868
  50.8 27.9 %collective-permute-start.2 = (bf16[512,512]{1,0:T(8,128)(2,1)S(1)}, bf16[512,512]{1,0:T(8,128)(2,1)S(1)}, u32[]{:S(2)}, u32[]{:S(2)}) collective-permute-start(bf16[512,512]{1,0:T(8,128)(2,1)S(1)} %collective-permute-done.1), channel_id=1, source_target_pairs={{0,4},{4,8},{8,12},{12,16},{16,20},{20,24},{24,28},{28,0},{1,5},{5... | collective-permute-start | bytes 1572872 | tf_op jit(solution)/shard_map/ppermute | solution.py:17
  78.7 87.4 %copy-start.6 = (bf16[512,512]{1,0:T(8,128)(2,1)}, bf16[512,512]{1,0:T(8,128)(2,1)S(1)}, u32[]{:S(2)}) copy-start(bf16[512,512]{1,0:T(8,128)(2,1)S(1)} %collective-permute-done.2) | copy-start | bytes 1572868
  78.7 18.3 %collective-permute-start.3 = (bf16[512,512]{1,0:T(8,128)(2,1)S(1)}, bf16[512,512]{1,0:T(8,128)(2,1)S(1)}, u32[]{:S(2)}, u32[]{:S(2)}) collective-permute-start(bf16[512,512]{1,0:T(8,128)(2,1)S(1)} %collective-permute-done.2), channel_id=1, source_target_pairs={{0,4},{4,8},{8,12},{12,16},{16,20},{20,24},{24,28},{28,0},{1,5},{5... | collective-permute-start | bytes 1572872 | tf_op jit(solution)/shard_map/ppermute | solution.py:17
  97.0 69.1 %copy-start.8 = (bf16[512,512]{1,0:T(8,128)(2,1)}, bf16[512,512]{1,0:T(8,128)(2,1)S(1)}, u32[]{:S(2)}) copy-start(bf16[512,512]{1,0:T(8,128)(2,1)S(1)} %collective-permute-done.3) | copy-start | bytes 1572868
  97.0 27.3 %collective-permute-start.4 = (bf16[512,512]{1,0:T(8,128)(2,1)S(1)}, bf16[512,512]{1,0:T(8,128)(2,1)S(1)}, u32[]{:S(2)}, u32[]{:S(2)}) collective-permute-start(bf16[512,512]{1,0:T(8,128)(2,1)S(1)} %collective-permute-done.3), channel_id=1, source_target_pairs={{0,4},{4,8},{8,12},{12,16},{16,20},{20,24},{24,28},{28,0},{1,5},{5... | collective-permute-start | bytes 1572872 | tf_op jit(solution)/shard_map/ppermute | solution.py:17
  124.3 41.9 %copy-start.10 = (bf16[512,512]{1,0:T(8,128)(2,1)}, bf16[512,512]{1,0:T(8,128)(2,1)S(1)}, u32[]{:S(2)}) copy-start(bf16[512,512]{1,0:T(8,128)(2,1)S(1)} %collective-permute-done.4) | copy-start | bytes 1572868
  124.3 27.6 %collective-permute-start.5 = (bf16[512,512]{1,0:T(8,128)(2,1)S(1)}, bf16[512,512]{1,0:T(8,128)(2,1)}, u32[]{:S(2)}, u32[]{:S(2)}) collective-permute-start(bf16[512,512]{1,0:T(8,128)(2,1)S(1)} %collective-permute-done.4), channel_id=1, source_target_pairs={{0,4},{4,8},{8,12},{12,16},{16,20},{20,24},{24,28},{28,0},{1,5},{5... | collective-permute-start | bytes 1572872 | tf_op jit(solution)/shard_map/ppermute | solution.py:17
  151.9 33.3 %collective-permute-start.6 = (bf16[512,512]{1,0:T(8,128)(2,1)}, bf16[512,512]{1,0:T(8,128)(2,1)}, u32[]{:S(2)}, u32[]{:S(2)}) collective-permute-start(bf16[512,512]{1,0:T(8,128)(2,1)} %collective-permute-done.5), channel_id=1, source_target_pairs={{0,4},{4,8},{8,12},{12,16},{16,20},{20,24},{24,28},{28,0},{1,5},{5... | collective-permute-start | bytes 1572872 | tf_op jit(solution)/shard_map/ppermute | solution.py:17
  166.9 27.0 %copy-start.11 = (bf16[512,512]{1,0:T(8,128)(2,1)S(1)}, bf16[512,512]{1,0:T(8,128)(2,1)}, u32[]{:S(2)}) copy-start(bf16[512,512]{1,0:T(8,128)(2,1)} %copy-done.10) | copy-start | bytes 1572868
  166.9 27.1 %copy-start.9 = (bf16[512,512]{1,0:T(8,128)(2,1)S(1)}, bf16[512,512]{1,0:T(8,128)(2,1)}, u32[]{:S(2)}) copy-start(bf16[512,512]{1,0:T(8,128)(2,1)} %copy-done.8) | copy-start | bytes 1572868
  166.9 27.1 %copy-start.7 = (bf16[512,512]{1,0:T(8,128)(2,1)S(1)}, bf16[512,512]{1,0:T(8,128)(2,1)}, u32[]{:S(2)}) copy-start(bf16[512,512]{1,0:T(8,128)(2,1)} %copy-done.6) | copy-start | bytes 1572868
  166.9 27.2 %copy-start.5 = (bf16[512,512]{1,0:T(8,128)(2,1)S(1)}, bf16[512,512]{1,0:T(8,128)(2,1)}, u32[]{:S(2)}) copy-start(bf16[512,512]{1,0:T(8,128)(2,1)} %copy-done.4) | copy-start | bytes 1572868
  166.9 30.6 %copy-start.1 = (bf16[2,128,4096]{2,1,0:T(8,128)(2,1)S(1)}, bf16[2,128,4096]{2,1,0:T(8,128)(2,1)}, u32[]{:S(2)}) copy-start(bf16[2,128,4096]{2,1,0:T(8,128)(2,1)} %param.6) | copy-start | bytes 6291460
  339.9 3.5 copy-start.12
  343.2 120.8 %reduce-scatter.3.cloned.1.call-start = ((), (), s32[]{:S(2)}) async-start(), calls=%async_computation.4 | async-start | bytes 2621440 | tf_op jit(solution)/shard_map/reduce_scatter | solution.py:101
  343.4 10.0 %slice-start = ((s8[8388608]{0:T(1024)(128)(4,1)}), s8[4194304]{0:T(1024)(128)(4,1)S(1)}, s32[]{:S(2)}) async-start(s8[8388608]{0:T(1024)(128)(4,1)} %bitcast.55), calls=%async_computation.6 | async-start | bytes 8388608
  346.5 6.9 %slice-start.1 = ((s8[8388608]{0:T(1024)(128)(4,1)}), s8[4194304]{0:T(1024)(128)(4,1)S(1)}, s32[]{:S(2)}) async-start(s8[8388608]{0:T(1024)(128)(4,1)} %bitcast.55), calls=%async_computation.7 | async-start | bytes 8388608
  (2 other events, 4.0 us)
Sparse Core Ops, SparseCore 0:
  10.0 178.9 all-gather.2
  191.0 131.3 all-gather.4
  343.3 86.8 reduce-scatter.4
  433.1 30.8 reduce-scatter.2
